TPU v7x, 32 devices: a whole 2x2x4 slice. The times are simulated.
32 devices in a mesh: cell: 2 (over x), blk: 16 (over z, y, core).
Axes of the slice: x: 2, y: 2, z: 4, core: 2. Of those that a mesh axis runs over, the one named last changes fastest.
Arguments:
- psi_val: float32 [256, 64, 64, 64], P('cell', 'blk'), parts along dimension 0, may hold values from -6 to 6
- psi_cond: float32 [6, 64, 64, 64], P('cell', 'blk'), parts along dimension 0, may hold values from -6 to 6
- e_val: float32 [256], P('cell'), parts along dimension 0, may hold values from -8 to -1
- e_cond: float32 [6], P('cell'), parts along dimension 0, may hold values from 1 to 8
- occ: int32 [256], P('cell'), parts along dimension 0, may hold values from 1 to 2
- freq: float32 [10], P('cell'), parts along dimension 0, may hold values from 0.5 to 16
- gmap: int32 [8192], P('cell'), parts along dimension 0, may hold values from 0 to 262143, as said below
Outputs:
- chi_real: float32 [10, 4096, 4096], P('cell', 'blk'), parts along dimension 0
- chi_imag: float32 [10, 4096, 4096], P('cell', 'blk'), parts along dimension 0
There are 2 independent parts, one for each index of `cell`. A program takes and returns all parts, laid end to end along the dimension named above; each array names one. Nothing has to cross between parts.
Inputs may be any that keep to these rules, and one draw needn't show every extreme that they name: `gmap`: the 4096 indices are distinct; index 0 and index 262143 are always among them.
All inputs are finite; a program needn't handle non-finite values.
Results may differ from a plain program's by a relative error of at most 0.0001.
Values sent between devices are 32-bit elements; how exact they have to be, the bound alone decides.
No kernel may reach another device: no remote copies, remote signals or barrier semaphores. Data moves between devices by JAX's collectives and lax.ppermute only.
A program may use at most 256 MiB of HBM per device.

v0:
```python
import math
import jax
import jax.numpy as jnp
from jax import lax
from jax.sharding import PartitionSpec as P

highest = lax.Precision.HIGHEST


def dft_tables(length):
    counter = jnp.arange(length, dtype=jnp.int32)
    angles = (counter[:, None] * counter[None, :] % length).astype(jnp.float32) * (
        2.0 * math.pi / length
    )
    return (jnp.cos(angles), jnp.sin(angles))


def plane_picks(val_part, cond_part, column_idx):
    num_val, planes, size_y, size_z = val_part.shape
    num_cond = cond_part.shape[0]
    pair_count = num_val * num_cond
    density = (val_part[:, None] * cond_part[None]).reshape(pair_count, planes, size_y, size_z)
    cos_z, sin_z = dft_tables(size_z)
    real_a = jnp.einsum("pxyz,zk->ykxp", density, cos_z, precision=highest)
    imag_a = -jnp.einsum("pxyz,zk->ykxp", density, sin_z, precision=highest)
    cos_y, sin_y = dft_tables(size_y)
    real_b = jnp.einsum("ly,ykxp->lkxp", cos_y, real_a, precision=highest) + jnp.einsum(
        "ly,ykxp->lkxp", sin_y, imag_a, precision=highest
    )
    imag_b = jnp.einsum("ly,ykxp->lkxp", cos_y, imag_a, precision=highest) - jnp.einsum(
        "ly,ykxp->lkxp", sin_y, real_a, precision=highest
    )
    return jnp.concatenate(
        [
            jnp.take(real_b.reshape(size_y * size_z, planes, pair_count), column_idx, axis=0),
            jnp.take(imag_b.reshape(size_y * size_z, planes, pair_count), column_idx, axis=0),
        ],
        axis=2,
    )


def phase_sum(values, freq_x, positions, size_x, norm_factor):
    half = values.shape[2] // 2
    angles = (freq_x[:, None] * positions[None, :] % size_x).astype(jnp.float32) * (
        2.0 * math.pi / size_x
    )
    cosine = jnp.cos(angles)[:, :, None]
    sine = jnp.sin(angles)[:, :, None]
    real_v = values[:, :, :half]
    imag_v = values[:, :, half:]
    real_m = jnp.sum(real_v * cosine + imag_v * sine, axis=1)
    imag_m = jnp.sum(imag_v * cosine - real_v * sine, axis=1)
    return jnp.concatenate([real_m, imag_m], axis=1) * norm_factor


def body(psi_val, psi_cond, e_val, e_cond, occ, freq, gmap):
    num_val, planes, size_y, size_z = psi_val.shape
    num_cond = psi_cond.shape[0]
    pairs = num_val * num_cond
    devices_blk = lax.axis_size("blk")
    size_x = planes * devices_blk
    total_points = size_x * size_y * size_z
    norm_factor = 1.0 / math.sqrt(total_points)
    column_idx = gmap % (size_y * size_z)
    plane_freq = gmap // (size_y * size_z)
    picked = plane_picks(psi_val, psi_cond, column_idx)
    positions = lax.axis_index("blk") * planes + jnp.arange(planes, dtype=jnp.int32)
    owned = lax.psum_scatter(
        phase_sum(picked, plane_freq, positions, size_x, norm_factor),
        "blk",
        scatter_dimension=0,
        tiled=True,
    )
    gaps = e_val[:, None] - e_cond[None, :]
    occ_col = occ.astype(jnp.float32)[:, None, None]
    weights = (
        occ_col
        * gaps[:, :, None]
        / (gaps[:, :, None] * gaps[:, :, None] + (freq * freq)[None, None, :])
    )
    weights = weights.reshape(pairs, freq.shape[0]) / math.sqrt(pairs)
    freq_weights = jnp.transpose(weights)[:, None, :]
    real_w = owned[None, :, :pairs] * freq_weights
    imag_w = owned[None, :, pairs:] * freq_weights
    left_side = jnp.stack(
        [jnp.concatenate([real_w, imag_w], axis=2), jnp.concatenate([imag_w, -real_w], axis=2)],
        axis=0,
    )
    chi_both = jnp.einsum(
        "awgk,hk->awgh",
        left_side,
        lax.all_gather(owned, "blk", axis=0, tiled=True),
        precision=highest,
    )
    return (chi_both[0], chi_both[1])


def solution(mesh):
    return jax.shard_map(
        body,
        mesh=mesh,
        in_specs=(
            P("cell", "blk", None, None),
            P("cell", "blk", None, None),
            P("cell"),
            P("cell"),
            P("cell"),
            P("cell"),
            P("cell"),
        ),
        out_specs=(P("cell", "blk", None), P("cell", "blk", None)),
        check_vma=False,
    )
```

profile of v0, /device:TPU:0, one launch (start us, length us, event | category | flops | bytes accessed | tf_op | source)
XLA Modules:
  0.0 1110.7 jit_solution(17548782149290452893)
XLA Ops:
  7.2 0.0 copy-start
  7.2 0.0 reduce-scatter.2.cloned.1.call-start
  7.2 16.3 %copy.40 = f32[128,4,64,64]{3,2,1,0:T(8,128)} copy(f32[128,4,64,64]{0,3,2,1:T(8,128)} %param.9) | data formatting | bytes 16777216 | tf_op args[0]
  23.5 0.0 copy-done
  23.5 23.2 %broadcast_multiply_fusion = f32[128,3,4,64,64]{4,3,2,1,0:T(8,128)} fusion(f32[3,4,64,64]{3,2,1,0:T(8,128)S(1)} %copy-done, f32[128,4,64,64]{3,2,1,0:T(8,128)} %copy.40), kind=kLoop, calls=%fused_computation.5 | loop fusion | flops 6291456 | bytes 33751040 | tf_op jit(solution)/shard_map/mul | solution.py:22
  46.7 40.4 %copy.42 = f32[384,4,64,64]{0,3,2,1:T(8,128)} copy(f32[384,4,64,64]{3,2,1,0:T(8,128)} %bitcast.45) | data formatting | bytes 50331648 | tf_op jit(solution)/shard_map/mul | solution.py:22
  87.1 29.5 %negate_bitcast_fusion = f32[64,64,4,384]{3,1,0,2:T(8,128)} fusion(f32[384,4,64,64]{0,3,2,1:T(8,128)} %copy.42), kind=kOutput, calls=%fused_computation.4 | convolution fusion | flops 4838187008 | bytes 50331648 | tf_op jit(solution)/shard_map/pxyz,zk->ykxp/dot_general | solution.py:25
  116.6 29.9 %convolution_bitcast_fusion = f32[64,64,4,384]{3,1,0,2:T(8,128)} fusion(f32[384,4,64,64]{0,3,2,1:T(8,128)} %copy.42), kind=kOutput, calls=%fused_computation.19 | convolution fusion | flops 4831895552 | bytes 50331648 | tf_op jit(solution)/shard_map/pxyz,zk->ykxp/dot_general | solution.py:24
  146.6 52.3 %fusion.2 = f32[64,64,4,384]{3,0,2,1:T(8,128)} fusion(f32[64,64,4,384]{3,1,0,2:T(8,128)} %negate_bitcast_fusion), kind=kOutput, calls=%fused_computation.8 | convolution fusion | flops 4831895552 | bytes 50331648 | tf_op jit(solution)/shard_map/ly,ykxp->lkxp/dot_general | solution.py:27
  198.9 0.0 copy-start.1
  198.9 51.7 %fusion = f32[64,64,4,384]{3,0,2,1:T(8,128)} fusion(f32[64,64,4,384]{3,1,0,2:T(8,128)} %negate_bitcast_fusion), kind=kOutput, calls=%fused_computation.6 | convolution fusion | flops 4831895552 | bytes 50331648 | tf_op jit(solution)/shard_map/ly,ykxp->lkxp/dot_general | solution.py:30
  250.7 0.0 copy-done.1
  250.7 54.9 %fusion.10 = f32[64,64,4,384]{3,0,2,1:T(8,128)} fusion(f32[64,64,4,384]{3,0,2,1:T(8,128)} %fusion.2, f32[64,64,4,384]{3,1,0,2:T(8,128)} %convolution_bitcast_fusion), kind=kOutput, calls=%fused_computation.20 | convolution fusion | flops 4838187008 | bytes 75497472 | tf_op jit(solution)/shard_map/ly,ykxp->lkxp/dot_general | solution.py:27
  305.7 21.8 %copy.47 = f32[64,64,4,384]{3,1,0,2:T(8,128)S(1)} copy(f32[64,64,4,384]{3,0,2,1:T(8,128)} %fusion.10) | data formatting | bytes 50331648 | tf_op jit(solution)/shard_map/add | solution.py:27
  327.5 59.9 %copy.48 = f32[4096,4,384]{2,1,0:T(4,128)} copy(f32[4096,4,384]{2,0,1:T(8,128)S(1)} %bitcast.46) | data formatting | bytes 50331648 | tf_op jit(solution)/shard_map/reshape | solution.py:35
  387.3 54.7 %fusion.13 = f32[64,64,4,384]{3,0,2,1:T(8,128)} fusion(f32[64,64,4,384]{3,0,2,1:T(8,128)} %fusion, f32[64,64,4,384]{3,1,0,2:T(8,128)} %convolution_bitcast_fusion), kind=kOutput, calls=%fused_computation.21 | convolution fusion | flops 4838187008 | bytes 75497472 | tf_op jit(solution)/shard_map/ly,ykxp->lkxp/dot_general | solution.py:30
  442.0 21.8 %copy.52 = f32[64,64,4,384]{3,1,0,2:T(8,128)S(1)} copy(f32[64,64,4,384]{3,0,2,1:T(8,128)} %fusion.13) | data formatting | bytes 50331648 | tf_op jit(solution)/shard_map/sub | solution.py:30
  463.8 59.8 %copy.53 = f32[4096,4,384]{2,1,0:T(4,128)} copy(f32[4096,4,384]{2,0,1:T(8,128)S(1)} %bitcast.47) | data formatting | bytes 50331648 | tf_op jit(solution)/shard_map/reshape | solution.py:36
  523.7 53.5 %gather_fusion = f32[4096,4,384]{2,1,0:T(4,128)} fusion(f32[4096,4,384]{2,1,0:T(4,128)} %copy.48, s32[4096]{0:T(1024)S(1)} %get-tuple-element.16), kind=kCustom, calls=%fused_computation.clone | custom fusion | bytes 50348032 | tf_op jit(solution)/shard_map/jit(_take)/gather | solution.py:35
  577.2 53.5 %gather_fusion.1 = f32[4096,4,384]{2,1,0:T(4,128)} fusion(f32[4096,4,384]{2,1,0:T(4,128)} %copy.53, s32[4096]{0:T(1024)S(1)} %get-tuple-element.16), kind=kCustom, calls=%fused_computation.1.clone | custom fusion | bytes 50348032 | tf_op jit(solution)/shard_map/jit(_take)/gather | solution.py:36
  630.7 0.6 fusion.33
  631.3 0.6 copy.49
  631.9 2.0 copy.54
  633.9 82.4 %add_reduce_fusion = (f32[4096,384]{1,0:T(8,128)}, f32[4096,384]{1,0:T(8,128)}) fusion(f32[4096,4,384]{2,1,0:T(4,128)} %gather_fusion.1, f32[4096,4,384]{2,1,0:T(4,128)} %gather_fusion, f32[4096,4]{1,0:T(8,128)} %copy.54, f32[4096,4]{1,0:T(8,128)S(1)} %copy.49, pred[4096]{0:T(1024)(128)(4,1)S(1)} %compare_and_fusion), kind=kLoop, calls=%fused_computation.3 | loop fusion | flops 59768832 | bytes 63049728 | tf_op jit(solution)/shard_map/reduce_sum | solution.py:51
  716.3 0.0 copy-start.4
  716.3 0.0 copy-start.2
  716.4 0.0 copy-start.3
  716.4 10.3 maximum_multiply_fusion
  726.7 0.0 reduce-scatter.2.cloned.1.call-update
  726.7 0.0 all-gather.2.cloned.1.call-start
  726.8 137.7 %reduce-scatter.2.cloned.1.call-done = f32[256,768]{1,0:T(8,128)} async-done(((f32[4096,768]{1,0:T(8,128)}), f32[256,768]{1,0:T(8,128)}) %reduce-scatter.2.cloned.1.call-update) | async-done | bytes 786448 | tf_op jit(solution)/shard_map/reduce_scatter | solution.py:68
  864.5 0.0 all-gather.2.cloned.1.call-update
  864.5 0.0 copy-done.4
  864.6 0.1 mul.224
  864.6 0.2 mul.225
  864.8 0.0 copy-done.2
  864.9 0.1 sub.39
  864.9 0.2 sub.40
  865.1 0.0 copy-done.3
  865.2 0.2 sub.42
  865.4 0.0 copy-done.5
  865.4 0.1 divide_multiply_fusion
  865.5 1.2 fusion.72
  866.7 0.5 broadcast_multiply_fusion.2
  867.2 3.9 maximum_bitcast_fusion
  871.1 95.4 %all-gather.2.cloned.1.call-done = f32[4096,768]{1,0:T(8,128)} async-done(((f32[256,768]{1,0:T(8,128)}), f32[4096,768]{1,0:T(8,128)}) %all-gather.2.cloned.1.call-update) | async-done | bytes 12582928 | tf_op jit(solution)/shard_map/all_gather | solution.py:92
  966.5 108.3 %fusion.8 = f32[2,5,256,4096]{3,2,1,0:T(8,128)} fusion(f32[4096,768]{1,0:T(8,128)} %all-gather.2.cloned.1.call-done, f32[1,5,256,768]{3,2,1,0:T(8,128)} %get-tuple-element.8, f32[1,5,256,768]{3,2,1,0:T(8,128)} %get-tuple-element.7), kind=kOutput, calls=%fused_computation.17 | convolution fusion | flops 96638730240 | bytes 62390272 | tf_op jit(solution)/shard_map/awgk,hk->awgh/dot_general | solution.py:89
  1074.8 28.8 %slice_bitcast_fusion = (f32[5,256,4096]{2,1,0:T(8,128)}, f32[5,256,4096]{2,1,0:T(8,128)}) fusion(f32[2,5,256,4096]{3,2,1,0:T(8,128)} %fusion.8), kind=kLoop, calls=%fused_computation.14 | loop fusion | bytes 83886080 | tf_op jit(solution)/shard_map/squeeze | solution.py:95
  (8 shorter events, 0.1 us)
Async XLA Ops:
  7.2 16.3 %copy-start = (f32[3,4,64,64]{3,2,1,0:T(8,128)S(1)}, f32[3,4,64,64]{3,2,1,0:T(8,128)}, u32[]{:S(2)}) copy-start(f32[3,4,64,64]{3,2,1,0:T(8,128)} %param.10) | copy-start | bytes 589828
  7.2 857.3 %reduce-scatter.2.cloned.1.call-start = ((), (), s32[]{:S(2)}) async-start(), calls=%async_computation.1 | async-start | bytes 13369344 | tf_op jit(solution)/shard_map/reduce_scatter | solution.py:68
  198.9 51.8 %copy-start.1 = (s32[4096]{0:T(1024)S(1)}, s32[4096]{0:T(1024)}, u32[]{:S(2)}) copy-start(s32[4096]{0:T(1024)} %param.15) | copy-start | bytes 49156
  716.3 148.2 %copy-start.4 = (s32[128]{0:T(128)S(1)}, s32[128]{0:T(128)}, u32[]{:S(2)}) copy-start(s32[128]{0:T(128)} %param.13) | copy-start | bytes 1540
  716.3 148.5 %copy-start.2 = (f32[128]{0:T(128)S(1)}, f32[128]{0:T(128)}, u32[]{:S(2)}) copy-start(f32[128]{0:T(128)} %param.11) | copy-start | bytes 1540
  716.4 148.8 %copy-start.3 = (f32[3]{0:T(128)S(1)}, f32[3]{0:T(128)}, u32[]{:S(2)}) copy-start(f32[3]{0:T(128)} %param.12) | copy-start | bytes 40
  716.4 149.0 %copy-start.5 = (f32[5]{0:T(128)S(1)}, f32[5]{0:T(128)}, u32[]{:S(2)}) copy-start(f32[5]{0:T(128)} %param.14) | copy-start | bytes 64
  726.7 239.8 %all-gather.2.cloned.1.call-start = ((), (), s32[]{:S(2)}) async-start(), calls=%async_computation.2 | async-start | bytes 13369344 | tf_op jit(solution)/shard_map/all_gather | solution.py:92
Sparse Core Ops, SparseCore 0:
  726.8 137.6 reduce-scatter.1
  866.8 99.6 all-gather.1
where the time goes:
time: 1120 us; the launch traced here: 1110 us
  matrix products  382 us (34%)
  local copies, waits for them, and re-layouts  360 us (32%)
  waiting for transfers between devices  233 us (21%)
  other arithmetic  121 us (11%)
  between operations  14.4 us (1%)
    reduce_scatter x1, waiting for transfers between devices, body(): lax.psum_scatter(phase_sum(picked, plane_freq, positions, size_x, norm_fa...  138 us
    dot_general x1, matrix products, body(): jnp.einsum('awgk,hk->awgh', left_side, lax.all_gather(owned, 'blk', axis=...  108 us
    all_gather x1, waiting for transfers between devices, body(): lax.all_gather(owned, 'blk', axis=0, tiled=True)  95.4 us
    reduce_sum x1, other arithmetic, phase_sum(): real_m = jnp.sum(real_v * cosine + imag_v * sine, axis=1)  82.4 us
    reshape x1, local copies, waits for them, and re-layouts, plane_picks(): real_b.reshape(size_y * size_z, planes, pair_count)  59.9 us
    reshape x1, local copies, waits for them, and re-layouts, plane_picks(): imag_b.reshape(size_y * size_z, planes, pair_count)  59.8 us
    dot_general x1, matrix products, plane_picks(): jnp.einsum('ly,ykxp->lkxp', cos_y, real_a, precision=highest)  54.9 us
    dot_general x1, matrix products, plane_picks(): jnp.einsum('ly,ykxp->lkxp', sin_y, real_a, precision=highest)  54.7 us
  transfers between devices with their start and end apart: 2, of which 2 were waited for; matrix products, arithmetic and copies ran while one was open for 1% of the time, Pallas kernels for 0%

commit v1 on v0

--- a/solution.py
+++ b/solution.py
@@ -89,7 +89,9 @@
     chi_both = jnp.einsum(
         "awgk,hk->awgh",
         left_side,
-        lax.all_gather(owned, "blk", axis=0, tiled=True),
+        jnp.concatenate(
+            lax.all_to_all(jnp.stack([owned] * lax.axis_size("blk")), "blk", 0, 0), axis=0
+        ),
         precision=highest,
     )
     return (chi_both[0], chi_both[1])

time: 1120 us -> 1300 us (1.16)
  the two profiles are of different devices: /device:TPU:0 before, /device:TPU:13 now
where the time goes in v1:
time: 1300 us; the launch traced here: 1290 us
  waiting for transfers between devices  402 us (31%)
  matrix products  382 us (29%)
  local copies, waits for them, and re-layouts  366 us (28%)
  other arithmetic  121 us (9%)
  between operations  14.4 us (1%)
    all_to_all x1, waiting for transfers between devices, body(): lax.all_to_all(jnp.stack([owned] * lax.axis_size('blk')), 'blk', 0, 0)  267 us
    reduce_scatter x1, waiting for transfers between devices, body(): lax.psum_scatter(phase_sum(picked, plane_freq, positions, size_x, norm_fa...  135 us
    dot_general x1, matrix products, body(): jnp.einsum('awgk,hk->awgh', left_side, jnp.concatenate(lax.all_to_all(jnp...  108 us
    reduce_sum x1, other arithmetic, phase_sum(): real_m = jnp.sum(real_v * cosine + imag_v * sine, axis=1)  82.4 us
    reshape x1, local copies, waits for them, and re-layouts, plane_picks(): real_b.reshape(size_y * size_z, planes, pair_count)  59.9 us
    reshape x1, local copies, waits for them, and re-layouts, plane_picks(): imag_b.reshape(size_y * size_z, planes, pair_count)  59.8 us
    dot_general x1, matrix products, plane_picks(): jnp.einsum('ly,ykxp->lkxp', cos_y, real_a, precision=highest)  54.9 us
    dot_general x1, matrix products, plane_picks(): jnp.einsum('ly,ykxp->lkxp', sin_y, real_a, precision=highest)  54.7 us
  transfers between devices with their start and end apart: 2, of which 2 were waited for; matrix products, arithmetic and copies ran while one was open for 0% of the time, Pallas kernels for 0%

profile of v1, /device:TPU:13, one launch (start us, length us, event | category | flops | bytes accessed | tf_op | source)
XLA Modules:
  0.0 1292.0 jit_solution(15202600187276450165)
XLA Ops:
  7.2 0.0 copy-start.1
  7.2 0.0 reduce-scatter.2.cloned.1.call-start
  7.2 16.3 %copy.40 = f32[128,4,64,64]{3,2,1,0:T(8,128)} copy(f32[128,4,64,64]{0,3,2,1:T(8,128)} %param.9) | data formatting | bytes 16777216 | tf_op args[0]
  23.5 0.0 copy-done.1
  23.5 23.2 %broadcast_multiply_fusion = f32[128,3,4,64,64]{4,3,2,1,0:T(8,128)} fusion(f32[3,4,64,64]{3,2,1,0:T(8,128)S(1)} %copy-done.1, f32[128,4,64,64]{3,2,1,0:T(8,128)} %copy.40), kind=kLoop, calls=%fused_computation.5 | loop fusion | flops 6291456 | bytes 33751040 | tf_op jit(solution)/shard_map/mul | solution.py:22
  46.7 40.4 %copy.42 = f32[384,4,64,64]{0,3,2,1:T(8,128)} copy(f32[384,4,64,64]{3,2,1,0:T(8,128)} %bitcast.46) | data formatting | bytes 50331648 | tf_op jit(solution)/shard_map/mul | solution.py:22
  87.1 29.5 %negate_bitcast_fusion = f32[64,64,4,384]{3,1,0,2:T(8,128)} fusion(f32[384,4,64,64]{0,3,2,1:T(8,128)} %copy.42), kind=kOutput, calls=%fused_computation.4 | convolution fusion | flops 4838187008 | bytes 50331648 | tf_op jit(solution)/shard_map/pxyz,zk->ykxp/dot_general | solution.py:25
  116.6 29.9 %convolution_bitcast_fusion = f32[64,64,4,384]{3,1,0,2:T(8,128)} fusion(f32[384,4,64,64]{0,3,2,1:T(8,128)} %copy.42), kind=kOutput, calls=%fused_computation.17 | convolution fusion | flops 4831895552 | bytes 50331648 | tf_op jit(solution)/shard_map/pxyz,zk->ykxp/dot_general | solution.py:24
  146.6 52.3 %fusion.2 = f32[64,64,4,384]{3,0,2,1:T(8,128)} fusion(f32[64,64,4,384]{3,1,0,2:T(8,128)} %negate_bitcast_fusion), kind=kOutput, calls=%fused_computation.8 | convolution fusion | flops 4831895552 | bytes 50331648 | tf_op jit(solution)/shard_map/ly,ykxp->lkxp/dot_general | solution.py:27
  198.9 0.0 copy-start.2
  198.9 51.7 %fusion = f32[64,64,4,384]{3,0,2,1:T(8,128)} fusion(f32[64,64,4,384]{3,1,0,2:T(8,128)} %negate_bitcast_fusion), kind=kOutput, calls=%fused_computation.6 | convolution fusion | flops 4831895552 | bytes 50331648 | tf_op jit(solution)/shard_map/ly,ykxp->lkxp/dot_general | solution.py:30
  250.7 0.0 copy-done.2
  250.7 54.9 %fusion.8 = f32[64,64,4,384]{3,0,2,1:T(8,128)} fusion(f32[64,64,4,384]{3,0,2,1:T(8,128)} %fusion.2, f32[64,64,4,384]{3,1,0,2:T(8,128)} %convolution_bitcast_fusion), kind=kOutput, calls=%fused_computation.18 | convolution fusion | flops 4838187008 | bytes 75497472 | tf_op jit(solution)/shard_map/ly,ykxp->lkxp/dot_general | solution.py:27
  305.7 21.8 %copy.47 = f32[64,64,4,384]{3,1,0,2:T(8,128)S(1)} copy(f32[64,64,4,384]{3,0,2,1:T(8,128)} %fusion.8) | data formatting | bytes 50331648 | tf_op jit(solution)/shard_map/add | solution.py:27
  327.5 59.9 %copy.48 = f32[4096,4,384]{2,1,0:T(4,128)} copy(f32[4096,4,384]{2,0,1:T(8,128)S(1)} %bitcast.47) | data formatting | bytes 50331648 | tf_op jit(solution)/shard_map/reshape | solution.py:35
  387.3 54.7 %fusion.11 = f32[64,64,4,384]{3,0,2,1:T(8,128)} fusion(f32[64,64,4,384]{3,0,2,1:T(8,128)} %fusion, f32[64,64,4,384]{3,1,0,2:T(8,128)} %convolution_bitcast_fusion), kind=kOutput, calls=%fused_computation.19 | convolution fusion | flops 4838187008 | bytes 75497472 | tf_op jit(solution)/shard_map/ly,ykxp->lkxp/dot_general | solution.py:30
  442.0 21.8 %copy.52 = f32[64,64,4,384]{3,1,0,2:T(8,128)S(1)} copy(f32[64,64,4,384]{3,0,2,1:T(8,128)} %fusion.11) | data formatting | bytes 50331648 | tf_op jit(solution)/shard_map/sub | solution.py:30
  463.8 59.8 %copy.53 = f32[4096,4,384]{2,1,0:T(4,128)} copy(f32[4096,4,384]{2,0,1:T(8,128)S(1)} %bitcast.48) | data formatting | bytes 50331648 | tf_op jit(solution)/shard_map/reshape | solution.py:36
  523.7 53.5 %gather_fusion = f32[4096,4,384]{2,1,0:T(4,128)} fusion(f32[4096,4,384]{2,1,0:T(4,128)} %copy.48, s32[4096]{0:T(1024)S(1)} %get-tuple-element.16), kind=kCustom, calls=%fused_computation.clone | custom fusion | bytes 50348032 | tf_op jit(solution)/shard_map/jit(_take)/gather | solution.py:35
  577.2 53.5 %gather_fusion.1 = f32[4096,4,384]{2,1,0:T(4,128)} fusion(f32[4096,4,384]{2,1,0:T(4,128)} %copy.53, s32[4096]{0:T(1024)S(1)} %get-tuple-element.16), kind=kCustom, calls=%fused_computation.1.clone | custom fusion | bytes 50348032 | tf_op jit(solution)/shard_map/jit(_take)/gather | solution.py:36
  630.7 0.6 fusion.32
  631.3 0.6 copy.49
  631.9 2.0 copy.54
  633.9 82.4 %add_reduce_fusion = (f32[4096,384]{1,0:T(8,128)}, f32[4096,384]{1,0:T(8,128)}) fusion(f32[4096,4,384]{2,1,0:T(4,128)} %gather_fusion.1, f32[4096,4,384]{2,1,0:T(4,128)} %gather_fusion, f32[4096,4]{1,0:T(8,128)} %copy.54, f32[4096,4]{1,0:T(8,128)S(1)} %copy.49, pred[4096]{0:T(1024)(128)(4,1)S(1)} %compare_and_fusion), kind=kLoop, calls=%fused_computation.3 | loop fusion | flops 59768832 | bytes 63049728 | tf_op jit(solution)/shard_map/reduce_sum | solution.py:51
  716.3 10.3 maximum_multiply_fusion
  726.6 0.0 copy-start.5
  726.6 0.0 copy-start.3
  726.6 0.0 reduce-scatter.2.cloned.1.call-update
  726.7 135.3 %reduce-scatter.2.cloned.1.call-done = f32[256,768]{1,0:T(8,128)} async-done(((f32[4096,768]{1,0:T(8,128)}), f32[256,768]{1,0:T(8,128)}) %reduce-scatter.2.cloned.1.call-update) | async-done | bytes 786448 | tf_op jit(solution)/shard_map/reduce_scatter | solution.py:68
  862.0 7.2 stack.11
  869.1 6.4 all-to-all-start
  875.6 0.0 copy-done.5
  875.6 0.1 mul.224
  875.7 0.2 mul.225
  875.9 0.0 copy-done.3
  875.9 0.1 sub.39
  876.0 0.2 sub.40
  876.2 0.0 copy-done.4
  876.2 0.2 sub.42
  876.4 0.0 copy-done.6
  876.4 0.1 divide_multiply_fusion
  876.5 0.0 copy-done
  876.5 0.1 fusion.71
  876.6 0.5 broadcast_multiply_fusion.2
  877.1 3.9 maximum_bitcast_fusion
  881.0 266.8 %all-to-all-done = f32[16,256,768]{2,1,0:T(8,128)} async-done(((f32[16,256,768]{2,1,0:T(8,128)}), f32[16,256,768]{2,1,0:T(8,128)}, u32[]{:S(2)}, u32[]{:S(2)}) %all-to-all-start) | async-done | bytes 12582944 | tf_op jit(solution)/shard_map/all_to_all | solution.py:93
  1147.8 108.3 %fusion.14 = f32[2,5,256,4096]{3,2,1,0:T(8,128)} fusion(f32[4096,768,1,1]{1,0,3,2:T(8,128)} %bitcast.17, f32[1,5,256,768]{3,2,1,0:T(8,128)} %get-tuple-element.8, f32[1,5,256,768]{3,2,1,0:T(8,128)} %get-tuple-element.7), kind=kOutput, calls=%fused_computation.20 | convolution fusion | flops 96638730240 | bytes 62390272 | tf_op jit(solution)/shard_map/awgk,hk->awgh/dot_general | solution.py:89
  1256.1 28.8 %slice_bitcast_fusion = (f32[5,256,4096]{2,1,0:T(8,128)}, f32[5,256,4096]{2,1,0:T(8,128)}) fusion(f32[2,5,256,4096]{3,2,1,0:T(8,128)} %fusion.14), kind=kLoop, calls=%fused_computation.14 | loop fusion | bytes 83886080 | tf_op jit(solution)/shard_map/squeeze | solution.py:97
  (10 shorter events, 0.1 us)
Async XLA Ops:
  7.2 16.3 %copy-start.1 = (f32[3,4,64,64]{3,2,1,0:T(8,128)S(1)}, f32[3,4,64,64]{3,2,1,0:T(8,128)}, u32[]{:S(2)}) copy-start(f32[3,4,64,64]{3,2,1,0:T(8,128)} %param.10) | copy-start | bytes 589828
  7.2 854.8 %reduce-scatter.2.cloned.1.call-start = ((), (), s32[]{:S(2)}) async-start(), calls=%async_computation.2 | async-start | bytes 13369344 | tf_op jit(solution)/shard_map/reduce_scatter | solution.py:68
  198.9 51.8 %copy-start.2 = (s32[4096]{0:T(1024)S(1)}, s32[4096]{0:T(1024)}, u32[]{:S(2)}) copy-start(s32[4096]{0:T(1024)} %param.15) | copy-start | bytes 49156
  726.6 148.9 %copy-start.5 = (s32[128]{0:T(128)S(1)}, s32[128]{0:T(128)}, u32[]{:S(2)}) copy-start(s32[128]{0:T(128)} %param.13) | copy-start | bytes 1540
  726.6 149.2 %copy-start.3 = (f32[128]{0:T(128)S(1)}, f32[128]{0:T(128)}, u32[]{:S(2)}) copy-start(f32[128]{0:T(128)} %param.11) | copy-start | bytes 1540
  726.6 149.5 %copy-start.4 = (f32[3]{0:T(128)S(1)}, f32[3]{0:T(128)}, u32[]{:S(2)}) copy-start(f32[3]{0:T(128)} %param.12) | copy-start | bytes 40
  726.6 149.8 %copy-start.6 = (f32[5]{0:T(128)S(1)}, f32[5]{0:T(128)}, u32[]{:S(2)}) copy-start(f32[5]{0:T(128)} %param.14) | copy-start | bytes 64
  861.9 14.6 %copy-start = (f32[256,768]{1,0:T(8,128)S(1)}, f32[256,768]{1,0:T(8,128)}, u32[]{:S(2)}) copy-start(f32[256,768]{1,0:T(8,128)} %reduce-scatter.2.cloned.1.call-done) | copy-start | bytes 2359300
  869.1 278.7 %all-to-all-start = ((f32[16,256,768]{2,1,0:T(8,128)}), f32[16,256,768]{2,1,0:T(8,128)}, u32[]{:S(2)}, u32[]{:S(2)}) async-start(f32[16,256,768]{2,1,0:T(8,128)} %stack.11), calls=%async_computation.1 | async-start | bytes 25165824 | tf_op jit(solution)/shard_map/all_to_all | solution.py:93
Sparse Core Ops, SparseCore 0:
  726.8 135.1 reduce-scatter.1
